TPU v7x, 512 devices: a whole 4x8x8 slice. The times are simulated.
512 devices in a mesh: head: 4 (over x), tensor: 16 (over y, z_hi), dp: 8 (over z_lo, core).
Axes of the slice: x: 4, y: 8, z: 8 (z_hi: 2, z_lo: 4; z = z_hi * 4 + z_lo), core: 2. Of those that a mesh axis runs over, the one named last changes fastest.
Arguments:
- trunk_hidden: bfloat16 [384, 5120], P('dp', 'tensor'), may hold values from -60 to 60
- next_embeds: bfloat16 [4, 384, 5120], P('head', 'dp', 'tensor'), may hold values from -6 to 6
- combine_weight: bfloat16 [4, 10240, 5120], P('head', 'dp', 'tensor'), may hold values from -0.0625 to 0.0625
- final_gain: float32 [5120], P('tensor'), may hold values from 0.5 to 1.5
- unembed_weight: bfloat16 [16384, 5120], P('dp', 'tensor'), may hold values from -32 to 32
- target_ids: int32 [4, 384], P('head'), may hold values from 0 to 16383
- loss_scale: float32 [4, 384], P('head'), may hold values from 2 to 32
Outputs:
- trunk_grad: float32 [384, 5120], P('dp', 'tensor')
- embed_grad: float32 [4, 384, 5120], P('head', 'dp', 'tensor')
- combine_grad: float32 [4, 10240, 5120], P('head', 'dp', 'tensor')
- unembed_grad: float32 [8, 4, 512, 5120], P('dp', 'head', None, 'tensor')
All inputs are finite; a program needn't handle non-finite values.
Results may differ from a plain program's by a relative error of at most 0.02.
Values may be sent and summed in bfloat16 or wider, within the bound.
A program may use at most 64 MiB of HBM per device.

v0:
```python
import jax
import jax.numpy as jnp
from jax import lax
from jax.sharding import PartitionSpec as P

D = 5120
epsilon = 1e-05


def contract_rows(left, right):
    return lax.dot_general(
        left, right, (((0,), (0,)), ((), ())), preferred_element_type=jnp.float32
    )


def contract_cols(left, right):
    return lax.dot_general(
        left, right, (((1,), (1,)), ((), ())), preferred_element_type=jnp.float32
    )


def local(
    trunk_hidden, next_embeds, combine_weight, final_gain, unembed_weight, target_ids, loss_scale
):
    rows, part_width = trunk_hidden.shape
    vocab_part = unembed_weight.shape[0]
    weight_block = combine_weight[0]
    trunk_whole, embed_whole = (
        lax.all_gather(trunk_hidden, "tensor", axis=1, tiled=True),
        lax.all_gather(next_embeds[0], "tensor", axis=1, tiled=True),
    )
    trunk_float = trunk_whole.astype(jnp.float32)
    embed_float = embed_whole.astype(jnp.float32)
    trunk_scale = lax.rsqrt(jnp.sum(trunk_float * trunk_float, axis=1) / D + epsilon)
    embed_scale = lax.rsqrt(jnp.sum(embed_float * embed_float, axis=1) / D + epsilon)
    trunk_normed = trunk_float * trunk_scale[:, None]
    embed_normed = embed_float * embed_scale[:, None]
    joined = jnp.concatenate(
        [trunk_normed.astype(jnp.bfloat16), embed_normed.astype(jnp.bfloat16)], axis=1
    )
    feature_start = lax.axis_index("tensor") * part_width
    trunk_local = lax.dynamic_slice_in_dim(trunk_normed, feature_start, part_width, 1)
    embed_local = lax.dynamic_slice_in_dim(embed_normed, feature_start, part_width, 1)
    blocks = lax.all_to_all(joined, "dp", split_axis=1, concat_axis=0, tiled=True)
    weight_whole = lax.all_gather(weight_block, "dp", axis=0, tiled=True)
    projected = jnp.dot(joined, weight_whole, preferred_element_type=jnp.float32)
    mixed = trunk_hidden.astype(jnp.float32) + projected
    mixed_sums = lax.psum(jnp.sum(mixed * mixed, axis=1), "tensor")
    mixed_scale = lax.rsqrt(mixed_sums / D + epsilon)
    mixed_normed = mixed * mixed_scale[:, None]
    normed_out = (mixed_normed * final_gain[None, :]).astype(jnp.bfloat16)
    normed_all = lax.all_gather(normed_out, "dp", axis=0, tiled=True)
    partial_logits = contract_cols(normed_all, unembed_weight)
    logits = lax.psum(partial_logits, "tensor")
    row_targets = target_ids[0]
    row_weights = loss_scale[0]
    largest = lax.pmax(jnp.max(logits, axis=1), "dp")
    shifted = jnp.exp(logits - largest[:, None])
    summed = lax.psum(jnp.sum(shifted, axis=1), "dp")
    probs = shifted / summed[:, None]
    vocab_ids = (
        lax.broadcasted_iota(jnp.int32, (1, vocab_part), 1) + lax.axis_index("dp") * vocab_part
    )
    hits = (vocab_ids == row_targets[:, None]).astype(jnp.float32)
    grad_local = (row_weights[:, None] * (probs - hits)).astype(jnp.bfloat16)
    grad_normed = lax.psum_scatter(
        jnp.dot(grad_local, unembed_weight, preferred_element_type=jnp.float32).astype(
            jnp.bfloat16
        ),
        "dp",
        scatter_dimension=0,
        tiled=True,
    ).astype(jnp.float32)
    vocab_term = contract_rows(grad_local, normed_all).astype(jnp.bfloat16)
    vocab_total = lax.psum_scatter(vocab_term, "head", scatter_dimension=0, tiled=True).astype(
        jnp.float32
    )
    unembed_grad = vocab_total.reshape(1, 1, vocab_total.shape[0], part_width)
    scaled_grad = grad_normed * final_gain[None, :]
    grad_dots = lax.psum(jnp.sum(scaled_grad * mixed_normed, axis=1), "tensor")
    grad_mixed = mixed_scale[:, None] * (scaled_grad - mixed_normed * (grad_dots / D)[:, None])
    grad_mixed_low = grad_mixed.astype(jnp.bfloat16)
    grad_all = lax.all_gather(grad_mixed_low, "dp", axis=0, tiled=True)
    combine_grad = contract_rows(blocks, grad_all)[None]
    joined_part = contract_cols(grad_mixed_low, weight_whole)
    joined_grad = lax.psum_scatter(
        joined_part.reshape(rows, 2, D).astype(jnp.bfloat16),
        "tensor",
        scatter_dimension=2,
        tiled=True,
    ).astype(jnp.float32)
    trunk_side = joined_grad[:, 0]
    embed_side = joined_grad[:, 1]
    trunk_dots, embed_dots = lax.psum(
        (jnp.sum(trunk_side * trunk_local, axis=1), jnp.sum(embed_side * embed_local, axis=1)),
        "tensor",
    )
    trunk_term = trunk_scale[:, None] * (trunk_side - trunk_local * (trunk_dots / D)[:, None])
    embed_grad = (embed_scale[:, None] * (embed_side - embed_local * (embed_dots / D)[:, None]))[
        None
    ]
    trunk_grad = lax.psum((grad_mixed + trunk_term).astype(jnp.bfloat16), "head").astype(
        jnp.float32
    )
    return (trunk_grad, embed_grad, combine_grad, unembed_grad)


def solution(mesh):
    in_specs = (
        P("dp", "tensor"),
        P("head", "dp", "tensor"),
        P("head", "dp", "tensor"),
        P("tensor"),
        P("dp", "tensor"),
        P("head", None),
        P("head", None),
    )
    out_specs = (
        P("dp", "tensor"),
        P("head", "dp", "tensor"),
        P("head", "dp", "tensor"),
        P("dp", "head", None, "tensor"),
    )
    return jax.shard_map(local, mesh=mesh, in_specs=in_specs, out_specs=out_specs, check_vma=False)
```

profile of v0, /device:TPU:32, one launch (start us, length us, event | category | flops | bytes accessed | tf_op | source)
XLA Modules:
  0.0 1121.4 jit_solution(15558136090920150623)
XLA Ops:
  8.0 69.0 %all-gather.2 = bf16[16,320,48]{1,2,0:T(8,128)(2,1)S(1)} all-gather(bf16[1,320,48]{1,2,0:T(8,128)(2,1)} %bitcast.77), channel_id=1, replica_groups=mesh['head'=4,'tensor'=16,'dp'=8] {'tensor'}, dimensions={0}, use_global_device_ids=true | all-gather | bytes 522240 | tf_op jit(solution)/shard_map/all_gather | solution.py:29
  77.6 160.0 %all-gather = bf16[1,48,5120]{1,0,2:T(2,128)(2,1)} all-gather(bf16[1,48,320]{1,0,2:T(2,128)(2,1)S(1)} %copy.16), channel_id=2, replica_groups=mesh['head'=4,'tensor'=16,'dp'=8] {'tensor'}, dimensions={2}, use_global_device_ids=true | all-gather | bytes 522240 | tf_op jit(solution)/shard_map/all_gather | solution.py:30
  237.6 4.7 copy.17
  245.2 5.1 multiply_reduce_fusion.3
  250.3 52.9 %psum.49 = f32[48]{0:T(128)S(1)} all-reduce(f32[48]{0:T(128)S(1)} %get-tuple-element.14), channel_id=1, replica_groups=mesh['head'=4,'tensor'=16,'dp'=8] {'tensor'}, use_global_device_ids=true, to_apply=%region_3.0 | all-reduce | flops 48 | bytes 384 | tf_op jit(solution)/shard_map/psum | solution.py:48
  303.3 17.8 %all_gather.18 = bf16[384,320]{1,0:T(8,128)(2,1)S(1)} all-gather(bf16[48,320]{1,0:T(8,128)(2,1)S(1)} %multiply_convert_fusion.1), channel_id=1, replica_groups=mesh['head'=4,'tensor'=16,'dp'=8] {'dp'}, dimensions={0}, use_global_device_ids=true | all-gather | bytes 276480 | tf_op jit(solution)/shard_map/all_gather | solution.py:52
  321.9 2.6 fusion.15
  325.3 340.8 %all-reduce.3.cloned.1.call-done = f32[384,2048]{1,0:T(8,128)} async-done(((f32[384,2048]{1,0:T(8,128)}), f32[384,2048]{1,0:T(8,128)}) %all-reduce.3.cloned.1.call-update) | async-done | bytes 3145744 | tf_op jit(solution)/shard_map/psum | solution.py:54
  668.2 13.6 %pmax.7 = f32[384]{0:T(512)S(1)} all-reduce(f32[384]{0:T(512)S(1)} %reduce_max.9), channel_id=1, replica_groups=mesh['head'=4,'tensor'=16,'dp'=8] {'dp'}, use_global_device_ids=true, to_apply=%region_6.0 | all-reduce | flops 384 | bytes 3072 | tf_op jit(solution)/shard_map/pmax | solution.py:57
  681.8 2.5 fusion.3
  684.3 13.6 %psum.51 = f32[384]{0:T(512)S(1)} all-reduce(f32[384]{0:T(512)S(1)} %fusion.3), channel_id=1, replica_groups=mesh['head'=4,'tensor'=16,'dp'=8] {'dp'}, use_global_device_ids=true, to_apply=%region_8.0 | all-reduce | flops 384 | bytes 3072 | tf_op jit(solution)/shard_map/psum | solution.py:59
  697.9 2.9 multiply_convert_fusion
  702.5 40.0 %reduce-scatter.6.cloned.1.call-done = bf16[48,320]{1,0:T(8,128)(2,1)} async-done(((bf16[384,320]{1,0:T(8,128)(2,1)}), bf16[48,320]{1,0:T(8,128)(2,1)}) %reduce-scatter.6.cloned.1.call-update) | async-done | bytes 30736 | tf_op jit(solution)/shard_map/reduce_scatter | solution.py:66
  743.4 49.8 %psum.52 = f32[48]{0:T(128)S(1)} all-reduce(f32[48]{0:T(128)S(1)} %multiply_reduce_fusion.2), channel_id=1, replica_groups=mesh['head'=4,'tensor'=16,'dp'=8] {'tensor'}, use_global_device_ids=true, to_apply=%region_11.0 | all-reduce | flops 48 | bytes 384 | tf_op jit(solution)/shard_map/psum | solution.py:80
  794.1 5.1 convolution_convert_fusion
  799.2 3.7 convert_element_type.64
  802.9 7.5 copy.20
  810.4 5.4 reshape.53
  815.8 2.9 convolution_convert_fusion.1
  820.9 3.6 all-to-all-start
  824.5 34.0 %all_gather.19 = bf16[384,320]{1,0:T(8,128)(2,1)S(1)} all-gather(bf16[48,320]{1,0:T(8,128)(2,1)S(1)} %fusion.13), channel_id=1, replica_groups=mesh['head'=4,'tensor'=16,'dp'=8] {'dp'}, dimensions={0}, use_global_device_ids=true | all-gather | bytes 276480 | tf_op jit(solution)/shard_map/all_gather | solution.py:83
  860.3 182.5 %reduce-scatter.10.cloned.1.call-done = bf16[320,96]{1,0:T(8,128)(2,1)} async-done(((bf16[5120,96]{1,0:T(8,128)(2,1)}), bf16[320,96]{1,0:T(8,128)(2,1)}) %reduce-scatter.10.cloned.1.call-update) | async-done | bytes 61456
  1045.1 48.3 %all-reduce = (f32[48]{0:T(128)S(1)}, f32[48]{0:T(128)S(1)}) all-reduce(f32[48]{0:T(128)S(1)} %get-tuple-element.5, f32[48]{0:T(128)S(1)} %get-tuple-element.4), channel_id=1, replica_groups=mesh['head'=4,'tensor'=16,'dp'=8] {'tensor'}, use_global_device_ids=true, to_apply=%region_14.0 | all-reduce | flops 96 | bytes 768 | tf_op jit(solution)/shard_map/psum | solution.py:94
  1095.1 17.3 %psum.54 = bf16[48,320]{1,0:T(8,128)(2,1)S(1)} all-reduce(bf16[48,320]{1,0:T(8,128)(2,1)S(1)} %get-tuple-element.13), channel_id=1, replica_groups=mesh['head'=4,'tensor'=16,'dp'=8] {'head'}, use_global_device_ids=true, to_apply=%region_15.0 | all-reduce | flops 15360 | bytes 61440 | tf_op jit(solution)/shard_map/psum | solution.py:102
  (61 shorter events, 22.0 us)
Async XLA Ops:
  7.2 314.8 %copy-start = (bf16[2048,320]{0,1:T(8,128)(2,1)S(1)}, bf16[2048,320]{0,1:T(8,128)(2,1)}, u32[]{:S(2)}) copy-start(bf16[2048,320]{0,1:T(8,128)(2,1)} %param.11) | copy-start | bytes 3932164
  7.2 70.2 %copy-start.5 = (bf16[1,48,320]{2,1,0:T(8,128)(2,1)S(1)}, bf16[1,48,320]{2,1,0:T(8,128)(2,1)}, u32[]{:S(2)}) copy-start(bf16[1,48,320]{2,1,0:T(8,128)(2,1)} %param.8) | copy-start | bytes 92164
  7.2 238.0 %all-gather.5.cloned.1.call-start = ((), (), s32[]{:S(2)}) async-start(), calls=%async_computation.7 | async-start | bytes 7372800 | tf_op jit(solution)/shard_map/all_gather | solution.py:45
  7.9 658.2 %all-reduce.3.cloned.1.call-start = ((), (), s32[]{:S(2)}) async-start(), calls=%async_computation.4 | async-start | bytes 6291456 | tf_op jit(solution)/shard_map/psum | solution.py:54
  242.6 2.6 copy-start.4
  245.1 5.2 copy-start.1
  245.2 58.1 %copy-start.6 = (f32[320]{0:T(512)S(1)}, f32[320]{0:T(512)}, u32[]{:S(2)}) copy-start(f32[320]{0:T(512)} %param.10) | copy-start | bytes 3844
  321.2 0.7 copy-start.2
  324.5 0.7 copy-start.7
  324.5 0.7 copy-start.8
  324.6 417.9 %reduce-scatter.6.cloned.1.call-start = ((), (), s32[]{:S(2)}) async-start(), calls=%async_computation.5 | async-start | bytes 331776 | tf_op jit(solution)/shard_map/reduce_scatter | solution.py:66
  702.5 340.3 %reduce-scatter.10.cloned.1.call-start = ((), (), s32[]{:S(2)}) async-start(), calls=%async_computation.8 | async-start | bytes 1392640
  815.8 297.2 %reduce-scatter.8.cloned.1.call-start = ((), (), s32[]{:S(2)}) async-start(), calls=%async_computation.6 | async-start | bytes 1638400 | tf_op jit(solution)/shard_map/reduce_scatter | solution.py:75
  820.9 37.6 %all-to-all-start = ((bf16[48,8,1280]{2,0,1:T(8,128)(2,1)}), bf16[48,8,1280]{2,0,1:T(8,128)(2,1)S(1)}, u32[]{:S(2)}, u32[]{:S(2)}) async-start(bf16[48,8,1280]{2,0,1:T(8,128)(2,1)} %bitcast.72), calls=%async_computation.1 | async-start | bytes 1966080 | tf_op jit(solution)/shard_map/all_to_all | solution.py:44
  824.4 268.9 %copy-start.3 = (bf16[48,320]{1,0:T(8,128)(2,1)S(1)}, bf16[48,320]{1,0:T(8,128)(2,1)}, u32[]{:S(2)}) copy-start(bf16[48,320]{1,0:T(8,128)(2,1)} %reduce-scatter.6.cloned.1.call-done) | copy-start | bytes 92164
Sparse Core Ops, SparseCore 0:
  10.1 162.1 all-gather.4
  324.7 341.3 all-reduce.2
  702.6 39.8 reduce-scatter.5
  815.9 226.8 reduce-scatter.9
  1045.5 26.0 reduce-scatter.7
where the time goes:
time: 1120 us
  waiting for transfers between devices  564 us (50%)
  blocking collectives  476 us (42%)
  local copies, waits for them, and re-layouts  25.4 us (2%)
  matrix products  19.3 us (2%)
  other arithmetic  18.7 us (2%)
  between operations  14 us (1%)
    psum x1, waiting for transfers between devices, local(): logits = lax.psum(partial_logits, 'tensor')  341 us
    unnamed x6, waiting for transfers between devices  183 us
    all_gather x1, blocking collectives, local(): lax.all_gather(next_embeds[0], 'tensor', axis=1, tiled=True)  160 us
    all_gather x1, blocking collectives, local(): lax.all_gather(trunk_hidden, 'tensor', axis=1, tiled=True)  69 us
    psum x1, blocking collectives, local(): mixed_sums = lax.psum(jnp.sum(mixed * mixed, axis=1), 'tensor')  52.9 us
    psum x1, blocking collectives, local(): grad_dots = lax.psum(jnp.sum(scaled_grad * mixed_normed, axis=1), 'tensor')  49.8 us
    psum x1, blocking collectives, local(): lax.psum((jnp.sum(trunk_side * trunk_local, axis=1), jnp.sum(embed_side *...  48.3 us
    reduce_scatter x1, waiting for transfers between devices, local(): lax.psum_scatter(jnp.dot(grad_local, unembed_weight, preferred_element_ty...  40 us
  transfers between devices with their start and end apart: 6, of which 3 were waited for; matrix products, arithmetic and copies ran while one was open for 2% of the time, Pallas kernels for 0%

commit v1 on v0

--- a/solution.py
+++ b/solution.py
@@ -27,7 +27,10 @@
     weight_block = combine_weight[0]
     trunk_whole, embed_whole = (
         lax.all_gather(trunk_hidden, "tensor", axis=1, tiled=True),
-        lax.all_gather(next_embeds[0], "tensor", axis=1, tiled=True),
+        jnp.concatenate(
+            lax.all_to_all(jnp.stack([next_embeds[0]] * lax.axis_size("tensor")), "tensor", 0, 0),
+            axis=1,
+        ),
     )
     trunk_float = trunk_whole.astype(jnp.float32)
     embed_float = embed_whole.astype(jnp.float32)

time: 1120 us -> 995 us (0.89)
  blocking collectives: 476 us -> 318 us
  starting transfers between devices: 3.76 us -> 19.4 us
  waiting for transfers between devices: 564 us -> 577 us
    all_gather x1 -> x0, blocking collectives: 160 us -> none  [local(): lax.all_gather(next_embeds[0], 'tensor', axis=1, tiled=True)]
    all_gather x1, waiting for transfers between devices: 0.01 us -> 18.7 us  [local(): weight_whole = lax.all_gather(weight_block, 'dp', axis=0, tiled=True)]
    all_to_all x0 -> x1, starting transfers between devices: none -> 15.7 us  [local(): lax.all_to_all(jnp.stack([next_embeds[0]] * lax.axis_size('tensor')), 'te...]
  transfers between devices with their start and end apart: 6 -> 7, of which waited for: 3 -> 4; matrix products, arithmetic and copies ran while one was open for 2% -> 2% of each run, Pallas kernels for 0% -> 0%
where the time goes in v1:
time: 995 us; the launch traced here: 994 us
  waiting for transfers between devices  577 us (58%)
  blocking collectives  318 us (32%)
  local copies, waits for them, and re-layouts  26.1 us (3%)
  other arithmetic  20.2 us (2%)
  starting transfers between devices  19.4 us (2%)
  matrix products  19.1 us (2%)
  between operations  13.9 us (1%)
    psum x1, waiting for transfers between devices, local(): logits = lax.psum(partial_logits, 'tensor')  334 us
    unnamed x6, waiting for transfers between devices  183 us
    all_gather x1, blocking collectives, local(): lax.all_gather(trunk_hidden, 'tensor', axis=1, tiled=True)  76.7 us
    psum x1, blocking collectives, local(): mixed_sums = lax.psum(jnp.sum(mixed * mixed, axis=1), 'tensor')  49.9 us
    psum x1, blocking collectives, local(): grad_dots = lax.psum(jnp.sum(scaled_grad * mixed_normed, axis=1), 'tensor')  49.9 us
    psum x1, blocking collectives, local(): lax.psum((jnp.sum(trunk_side * trunk_local, axis=1), jnp.sum(embed_side *...  48.3 us
    reduce_scatter x1, waiting for transfers between devices, local(): lax.psum_scatter(jnp.dot(grad_local, unembed_weight, preferred_element_ty...  41.4 us
    all_gather x1, blocking collectives, local(): grad_all = lax.all_gather(grad_mixed_low, 'dp', axis=0, tiled=True)  34.1 us
  transfers between devices with their start and end apart: 7, of which 4 were waited for; matrix products, arithmetic and copies ran while one was open for 2% of the time, Pallas kernels for 0%

profile of v1, /device:TPU:32, one launch (start us, length us, event | category | flops | bytes accessed | tf_op | source)
XLA Modules:
  0.0 993.7 jit_solution(7290781713229587160)
XLA Ops:
  9.6 15.7 %all-to-all-start = ((bf16[16,48,320]{2,1,0:T(8,128)(2,1)}), bf16[16,48,320]{2,1,0:T(8,128)(2,1)S(1)}, u32[]{:S(2)}, u32[]{:S(2)}) async-start(bf16[16,48,320]{2,1,0:T(8,128)(2,1)} %stack.3), calls=%async_computation | async-start | bytes 1179648 | tf_op jit(solution)/shard_map/all_to_all | solution.py:31
  25.3 76.7 %all-gather.1 = bf16[16,320,48]{1,2,0:T(8,128)(2,1)S(1)} all-gather(bf16[1,320,48]{1,2,0:T(8,128)(2,1)S(1)} %bitcast.74), channel_id=1, replica_groups=mesh['head'=4,'tensor'=16,'dp'=8] {'tensor'}, dimensions={0}, use_global_device_ids=true | all-gather | bytes 522240 | tf_op jit(solution)/shard_map/all_gather | solution.py:29
  110.7 18.7 %all-gather.4.cloned.1.call-done = bf16[1,10240,320]{1,2,0:T(8,128)(2,1)} async-done(((bf16[1,1280,320]{1,2,0:T(8,128)(2,1)}), bf16[1,10240,320]{1,2,0:T(8,128)(2,1)}) %all-gather.4.cloned.1.call-update) | async-done | bytes 6553616 | tf_op jit(solution)/shard_map/all_gather | solution.py:48
  129.4 5.0 multiply_reduce_fusion.3
  134.4 49.9 %psum.49 = f32[48]{0:T(128)S(1)} all-reduce(f32[48]{0:T(128)S(1)} %get-tuple-element.14), channel_id=1, replica_groups=mesh['head'=4,'tensor'=16,'dp'=8] {'tensor'}, use_global_device_ids=true, to_apply=%region_3.0 | all-reduce | flops 48 | bytes 384 | tf_op jit(solution)/shard_map/psum | solution.py:51
  184.4 14.3 %all_gather.14 = bf16[384,320]{1,0:T(8,128)(2,1)S(1)} all-gather(bf16[48,320]{1,0:T(8,128)(2,1)S(1)} %multiply_convert_fusion.1), channel_id=1, replica_groups=mesh['head'=4,'tensor'=16,'dp'=8] {'dp'}, dimensions={0}, use_global_device_ids=true | all-gather | bytes 276480 | tf_op jit(solution)/shard_map/all_gather | solution.py:55
  199.4 2.6 fusion.15
  202.7 334.4 %all-reduce.3.cloned.1.call-done = f32[384,2048]{1,0:T(8,128)} async-done(((f32[384,2048]{1,0:T(8,128)}), f32[384,2048]{1,0:T(8,128)}) %all-reduce.3.cloned.1.call-update) | async-done | bytes 3145744 | tf_op jit(solution)/shard_map/psum | solution.py:57
  539.2 13.6 %pmax.7 = f32[384]{0:T(512)S(1)} all-reduce(f32[384]{0:T(512)S(1)} %reduce_max.9), channel_id=1, replica_groups=mesh['head'=4,'tensor'=16,'dp'=8] {'dp'}, use_global_device_ids=true, to_apply=%region_6.0 | all-reduce | flops 384 | bytes 3072 | tf_op jit(solution)/shard_map/pmax | solution.py:60
  552.8 2.5 fusion.3
  555.2 13.6 %psum.51 = f32[384]{0:T(512)S(1)} all-reduce(f32[384]{0:T(512)S(1)} %fusion.3), channel_id=1, replica_groups=mesh['head'=4,'tensor'=16,'dp'=8] {'dp'}, use_global_device_ids=true, to_apply=%region_8.0 | all-reduce | flops 384 | bytes 3072 | tf_op jit(solution)/shard_map/psum | solution.py:62
  568.8 2.9 multiply_convert_fusion
  573.5 41.4 %reduce-scatter.6.cloned.1.call-done = bf16[48,320]{1,0:T(8,128)(2,1)} async-done(((bf16[384,320]{1,0:T(8,128)(2,1)}), bf16[48,320]{1,0:T(8,128)(2,1)}) %reduce-scatter.6.cloned.1.call-update) | async-done | bytes 30736 | tf_op jit(solution)/shard_map/reduce_scatter | solution.py:69
  615.9 49.9 %psum.52 = f32[48]{0:T(128)S(1)} all-reduce(f32[48]{0:T(128)S(1)} %multiply_reduce_fusion.2), channel_id=1, replica_groups=mesh['head'=4,'tensor'=16,'dp'=8] {'tensor'}, use_global_device_ids=true, to_apply=%region_11.0 | all-reduce | flops 48 | bytes 384 | tf_op jit(solution)/shard_map/psum | solution.py:83
  666.6 5.1 convolution_convert_fusion
  671.7 3.7 convert_element_type.77
  675.4 7.5 copy.19
  682.8 5.4 reshape.57
  688.3 2.9 convolution_convert_fusion.1
  693.3 3.6 all-to-all-start.1
  696.9 34.1 %all_gather.15 = bf16[384,320]{1,0:T(8,128)(2,1)S(1)} all-gather(bf16[48,320]{1,0:T(8,128)(2,1)S(1)} %fusion.13), channel_id=1, replica_groups=mesh['head'=4,'tensor'=16,'dp'=8] {'dp'}, dimensions={0}, use_global_device_ids=true | all-gather | bytes 276480 | tf_op jit(solution)/shard_map/all_gather | solution.py:86
  732.8 182.2 %reduce-scatter.10.cloned.1.call-done = bf16[320,96]{1,0:T(8,128)(2,1)} async-done(((bf16[5120,96]{1,0:T(8,128)(2,1)}), bf16[320,96]{1,0:T(8,128)(2,1)}) %reduce-scatter.10.cloned.1.call-update) | async-done | bytes 61456
  917.3 48.3 %all-reduce = (f32[48]{0:T(128)S(1)}, f32[48]{0:T(128)S(1)}) all-reduce(f32[48]{0:T(128)S(1)} %get-tuple-element.5, f32[48]{0:T(128)S(1)} %get-tuple-element.4), channel_id=1, replica_groups=mesh['head'=4,'tensor'=16,'dp'=8] {'tensor'}, use_global_device_ids=true, to_apply=%region_14.0 | all-reduce | flops 96 | bytes 768 | tf_op jit(solution)/shard_map/psum | solution.py:97
  967.3 17.3 %psum.54 = bf16[48,320]{1,0:T(8,128)(2,1)S(1)} all-reduce(bf16[48,320]{1,0:T(8,128)(2,1)S(1)} %get-tuple-element.13), channel_id=1, replica_groups=mesh['head'=4,'tensor'=16,'dp'=8] {'head'}, use_global_device_ids=true, to_apply=%region_15.0 | all-reduce | flops 15360 | bytes 61440 | tf_op jit(solution)/shard_map/psum | solution.py:105
  (64 shorter events, 28.9 us)
Async XLA Ops:
  7.2 192.2 %copy-start = (bf16[2048,320]{0,1:T(8,128)(2,1)S(1)}, bf16[2048,320]{0,1:T(8,128)(2,1)}, u32[]{:S(2)}) copy-start(bf16[2048,320]{0,1:T(8,128)(2,1)} %param.11) | copy-start | bytes 3932164
  7.2 18.1 %copy-start.5 = (bf16[48,320]{1,0:T(8,128)(2,1)S(1)}, bf16[48,320]{1,0:T(8,128)(2,1)}, u32[]{:S(2)}) copy-start(bf16[48,320]{1,0:T(8,128)(2,1)} %param.7) | copy-start | bytes 92164
  7.2 122.2 %all-gather.4.cloned.1.call-start = ((), (), s32[]{:S(2)}) async-start(), calls=%async_computation.8 | async-start | bytes 7372800 | tf_op jit(solution)/shard_map/all_gather | solution.py:48
  9.6 96.7 %all-to-all-start = ((bf16[16,48,320]{2,1,0:T(8,128)(2,1)}), bf16[16,48,320]{2,1,0:T(8,128)(2,1)S(1)}, u32[]{:S(2)}, u32[]{:S(2)}) async-start(bf16[16,48,320]{2,1,0:T(8,128)(2,1)} %stack.3), calls=%async_computation | async-start | bytes 1179648 | tf_op jit(solution)/shard_map/all_to_all | solution.py:31
  25.2 511.9 %all-reduce.3.cloned.1.call-start = ((), (), s32[]{:S(2)}) async-start(), calls=%async_computation.5 | async-start | bytes 6291456 | tf_op jit(solution)/shard_map/psum | solution.py:57
  108.1 21.3 %copy-start.1 = (bf16[48,5120]{1,0:T(8,128)(2,1)S(1)}, bf16[48,5120]{1,0:T(8,128)(2,1)}, u32[]{:S(2)}) copy-start(bf16[48,5120]{1,0:T(8,128)(2,1)} %get-tuple-element.8) | copy-start | bytes 1474564
  110.7 23.6 %copy-start.2 = (bf16[48,5120]{1,0:T(8,128)(2,1)}, bf16[48,5120]{1,0:T(8,128)(2,1)S(1)}, u32[]{:S(2)}) copy-start(bf16[48,5120]{1,0:T(8,128)(2,1)S(1)} %get-tuple-element.10) | copy-start | bytes 1474564
  129.4 54.9 %copy-start.6 = (f32[320]{0:T(512)S(1)}, f32[320]{0:T(512)}, u32[]{:S(2)}) copy-start(f32[320]{0:T(512)} %param.10) | copy-start | bytes 3844
  198.6 0.7 copy-start.3
  202.0 0.7 copy-start.7
  202.0 0.7 copy-start.8
  202.0 412.9 %reduce-scatter.6.cloned.1.call-start = ((), (), s32[]{:S(2)}) async-start(), calls=%async_computation.6 | async-start | bytes 331776 | tf_op jit(solution)/shard_map/reduce_scatter | solution.py:69
  573.5 341.5 %reduce-scatter.10.cloned.1.call-start = ((), (), s32[]{:S(2)}) async-start(), calls=%async_computation.9 | async-start | bytes 1392640
  688.2 297.0 %reduce-scatter.8.cloned.1.call-start = ((), (), s32[]{:S(2)}) async-start(), calls=%async_computation.7 | async-start | bytes 1638400 | tf_op jit(solution)/shard_map/reduce_scatter | solution.py:78
  693.3 37.7 %all-to-all-start.1 = ((bf16[48,8,1280]{2,0,1:T(8,128)(2,1)}), bf16[48,8,1280]{2,0,1:T(8,128)(2,1)S(1)}, u32[]{:S(2)}, u32[]{:S(2)}) async-start(bf16[48,8,1280]{2,0,1:T(8,128)(2,1)} %bitcast.69), calls=%async_computation.2 | async-start | bytes 1966080 | tf_op jit(solution)/shard_map/all_to_all | solution.py:47
  731.0 234.6 %copy-start.4 = (bf16[48,320]{1,0:T(8,128)(2,1)S(1)}, bf16[48,320]{1,0:T(8,128)(2,1)}, u32[]{:S(2)}) copy-start(bf16[48,320]{1,0:T(8,128)(2,1)} %reduce-scatter.6.cloned.1.call-done) | copy-start | bytes 92164
Sparse Core Ops, SparseCore 0:
  10.1 119.2 all-gather.3
  202.1 334.9 all-reduce.2
  573.6 41.2 reduce-scatter.5
  688.4 226.5 reduce-scatter.9
  917.7 25.9 reduce-scatter.7
